TPU v7x, 32 devices: a whole 2x2x4 slice. The times are simulated.
32 devices in a mesh: groups: 2 (over x), grid: 16 (over z, y, core).
Axes of the slice: x: 2, y: 2, z: 4, core: 2. Of those that a mesh axis runs over, the one named last changes fastest.
Arguments:
- hist: float32 [768, 256, 256], P('groups', 'grid'), parts along dimension 0, may hold values from 0.2 to 2
- drift: float32 [2, 256, 256], P(None, 'grid'), may hold values from -0.5 to 0.5
- shocks: int32 [768, 2], P('groups'), parts along dimension 0, may hold values from 0 to 7
- shock_table: float32 [16, 2], P('groups'), parts along dimension 0, may hold values from -0.3 to 0.3
- first_weight: bfloat16 [131072, 2048], P(('groups', 'grid')), parts along dimension 0, may hold values from -0.03125 to 0.03125
- mid_weight: bfloat16 [4096, 2048], P('groups', 'grid'), parts along dimension 0, may hold values from -0.1875 to 0.1875
- head_weight: float32 [4096], P(('groups', 'grid')), parts along dimension 0, may hold values from -0.125 to 0.125
- cotangent: float32 [768], P('groups'), parts along dimension 0, may hold values from -6 to 6
Outputs:
- hist_next: float32 [768, 256, 256], P('groups', 'grid'), parts along dimension 0
- value: float32 [768], P('groups'), parts along dimension 0
- grad_first: bfloat16 [131072, 2048], P(('groups', 'grid')), parts along dimension 0
- grad_mid: bfloat16 [4096, 2048], P('groups', 'grid'), parts along dimension 0
- grad_head: float32 [4096], P(('groups', 'grid')), parts along dimension 0
There are 2 independent parts, one for each index of `groups`. A program takes and returns all parts, laid end to end along the dimension named above; an argument that names none is the same for every part. Nothing has to cross between parts.
All inputs are finite; a program needn't handle non-finite values.
Results may differ from a plain program's by a relative error of at most 0.0173.
Values may be sent and summed in bfloat16 or wider, within the bound.
A program may use at most 128 MiB of HBM per device.

v0:
```python
import jax
import jax.numpy as jnp
from jax import lax
from jax.sharding import PartitionSpec as P

diffusion_rate = 0.24


def padded_2(block, sides, width):
    for axis, dim in sides:
        count = lax.axis_size(axis)
        forward = [(i, i + 1) for i in range(count - 1)]
        backward = [(target, source) for source, target in forward]
        low = lax.ppermute(
            lax.slice_in_dim(block, block.shape[dim] - width, None, axis=dim), axis, forward
        )
        high = lax.ppermute(lax.slice_in_dim(block, 0, width, axis=dim), axis, backward)
        block = jnp.concatenate([low, block, high], axis=dim)
    return block


def column_shift(values, offset):
    zero_col = jnp.zeros_like(values[..., :1])
    if offset > 0:
        return jnp.concatenate([values[..., 1:], zero_col], axis=-1)
    return jnp.concatenate([zero_col, values[..., :-1]], axis=-1)


def shock_shift(levels_now, table):
    level_ids = lax.iota(jnp.int32, table.shape[0])
    onehot = (levels_now[:, None] == level_ids[None, :]).astype(jnp.float32)
    return jnp.sum(onehot[:, :, None] * table[None, :, :], axis=1)


def kfe_step(padded, drift_rows, shift_x, shift_y):
    velocity_x = drift_rows[0][None] + shift_x[:, None, None]
    velocity_y = drift_rows[1][1:-1][None] + shift_y[:, None, None]
    flux_x = velocity_x * padded
    centre = padded[:, 1:-1]
    flux_y = velocity_y * centre
    spread = (
        padded[:, 2:]
        + padded[:, :-2]
        + column_shift(centre, 1)
        + column_shift(centre, -1)
        - 4.0 * centre
    )
    carried = 0.5 * (flux_x[:, 2:] - flux_x[:, :-2]) + 0.5 * (
        column_shift(flux_y, 1) - column_shift(flux_y, -1)
    )
    return centre + diffusion_rate * spread - carried


def local(hist, drift, shocks, shock_table, first_weight, mid_weight, head_weight, cotangent):
    scenarios, row_count, columns = hist.shape
    step_count = shocks.shape[1]
    density = hist
    drift_ext = padded_2(drift, (("grid", 1),), 1)
    for section_no in range(step_count):
        shifts = shock_shift(shocks[:, section_no], shock_table)
        padded = padded_2(density, (("grid", 1),), 1)
        density = kfe_step(padded, drift_ext, shifts[:, 0], shifts[:, 1])
    inputs = density.astype(jnp.bfloat16).reshape(scenarios, row_count * columns)
    partial_first = jnp.dot(inputs, first_weight, preferred_element_type=jnp.float32)
    first_pre = lax.psum(partial_first, "grid")
    first_act = jnp.tanh(first_pre).astype(jnp.bfloat16)
    second_pre = jnp.dot(first_act, mid_weight, preferred_element_type=jnp.float32)
    second_act = jnp.tanh(second_pre).astype(jnp.bfloat16)
    second_f = second_act.astype(jnp.float32)
    value_part = jnp.dot(second_f, head_weight, precision=lax.Precision.HIGHEST)
    value = lax.psum(value_part, "grid")
    grad_head = jnp.dot(cotangent, second_f, precision=lax.Precision.HIGHEST)
    back_second = (cotangent[:, None] * head_weight[None, :] * (1.0 - second_f * second_f)).astype(
        jnp.bfloat16
    )
    grad_mid = lax.dot_general(
        first_act, back_second, (((0,), (0,)), ((), ())), preferred_element_type=jnp.float32
    )
    back_part = lax.dot_general(
        back_second, mid_weight, (((1,), (1,)), ((), ())), preferred_element_type=jnp.float32
    )
    back_raw = lax.psum(back_part, "grid")
    first_f = first_act.astype(jnp.float32)
    back_first = (back_raw * (1.0 - first_f * first_f)).astype(jnp.bfloat16)
    grad_first = lax.dot_general(
        inputs, back_first, (((0,), (0,)), ((), ())), preferred_element_type=jnp.float32
    )
    return (
        density,
        value,
        grad_first.astype(jnp.bfloat16),
        grad_mid.astype(jnp.bfloat16),
        grad_head,
    )


def solution(mesh):
    in_specs = (
        P("groups", "grid", None),
        P(None, "grid", None),
        P("groups", None),
        P("groups", None),
        P(("groups", "grid"), None),
        P("groups", "grid"),
        P(("groups", "grid")),
        P("groups"),
    )
    out_specs = (
        P("groups", "grid", None),
        P("groups"),
        P(("groups", "grid"), None),
        P("groups", "grid"),
        P(("groups", "grid")),
    )
    return jax.shard_map(local, mesh=mesh, in_specs=in_specs, out_specs=out_specs, check_vma=False)
```

profile of v0, /device:TPU:0, one launch (start us, length us, event | category | flops | bytes accessed | tf_op | source)
XLA Modules:
  0.0 387.2 jit_solution(2880481211151766229)
XLA Ops:
  7.2 0.0 copy-start
  7.2 0.0 all-reduce.11.cloned.1.call-start
  7.2 0.8 fusion.37
  8.0 2.4 collective-permute-start.2
  10.4 1.3 collective-permute-start.3
  11.7 3.4 fusion.35
  15.1 1.3 collective-permute-start
  16.4 0.8 copy.71
  17.2 6.7 %collective-permute-start.1 = (f32[384,1,256]{2,0,1:T(8,128)}, f32[384,1,256]{2,0,1:T(8,128)}, u32[]{:S(2)}, u32[]{:S(2)}) collective-permute-start(f32[384,1,256]{2,0,1:T(8,128)} %copy.71), channel_id=1, source_target_pairs={{0,1},{1,2},{2,3},{3,4},{4,5},{5,6},{6,7},{7,8},{8,9},{9,10},{10,1... | collective-permute-start | bytes 1179656 | tf_op jit(solution)/shard_map/ppermute | solution.py:14
  23.9 6.6 %copy.58 = f32[384,16,256]{0,2,1:T(8,128)} copy(f32[384,16,256]{2,1,0:T(8,128)} %param.8) | data formatting | bytes 12582912 | tf_op args[0]
  30.5 0.1 multiply_reduce_fusion
  30.7 10.8 %fusion.34 = (f32[384,16,255]{0,2,1:T(8,128)}, f32[384,16,255]{0,2,1:T(8,128)}) fusion(f32[384,16,256]{0,2,1:T(8,128)} %copy.58), kind=kLoop, calls=%fused_computation.63 | loop fusion | bytes 25067520 | tf_op jit(solution)/shard_map/slice | solution.py:25
  41.4 4.9 %add_multiply_fusion.1 = f32[384,16,256]{0,2,1:T(8,128)} fusion(f32[384,16,256]{0,2,1:T(8,128)} %copy.58, f32[384]{0:T(512)S(1)} %get-tuple-element.24, f32[16,256]{1,0:T(8,128)S(1)} %slice_bitcast_fusion), kind=kLoop, calls=%fused_computation.28 | loop fusion | flops 3145728 | bytes 12600832 | tf_op jit(solution)/shard_map/mul | solution.py:40
  46.4 10.8 %fusion.36 = (f32[384,16,255]{0,2,1:T(8,128)}, f32[384,16,255]{0,2,1:T(8,128)}) fusion(f32[384,16,256]{0,2,1:T(8,128)} %add_multiply_fusion.1), kind=kLoop, calls=%fused_computation.65 | loop fusion | bytes 25067520 | tf_op jit(solution)/shard_map/slice | solution.py:25
  57.2 0.0 slice-start
  57.2 0.2 copy.51
  57.4 1.3 copy.53
  58.7 6.0 %maximum_multiply_fusion = f32[384,18,256]{0,2,1:T(8,128)} fusion(f32[384,1,256]{0,2,1:T(8,128)S(1)} %copy.51, f32[384,16,256]{0,2,1:T(8,128)} %copy.58, f32[384,1,256]{0,2,1:T(8,128)S(1)} %copy.53, f32[384]{0:T(512)S(1)} %get-tuple-element.25, f32[18,256]{1,0:T(8,128)S(1)} %fusion.20), kind=kLoop, calls=%fused_computation.1 | loop fusion | flops 7077888 | bytes 14175744 | tf_op jit(solution)/shard_map/mul | solution.py:38
  64.8 2.4 slice-done.1
  67.2 14.2 %add_multiply_fusion = (f32[384,16,256]{0,2,1:T(8,128)}, f32[384,16,256]{0,2,1:T(8,128)S(1)}) fusion(f32[384]{0:T(512)S(1)} %get-tuple-element.20, f32[16,256]{1,0:T(8,128)S(1)} %slice_bitcast_fusion, f32[384,16,255]{0,2,1:T(8,128)} %get-tuple-element.43, f32[384,16,255]{0,2,1:T(8,128)} %get-tuple-element.42, f32[384,18,256]{0,2,1:T(8,128)} %maximum_multiply_fusion, ...), kind=kLoop, calls=%fused_computation.27 | loop fusion | flops 25165824 | bytes 57329152 | tf_op jit(solution)/shard_map/mul | solution.py:40
  81.4 2.6 copy-done.1
  84.0 0.1 fusion.32
  84.1 10.8 %fusion.31 = (f32[384,16,255]{0,2,1:T(8,128)}, f32[384,16,255]{0,2,1:T(8,128)}) fusion(f32[384,16,256]{0,2,1:T(8,128)} %copy-done.1), kind=kLoop, calls=%fused_computation.60 | loop fusion | bytes 25067520 | tf_op jit(solution)/shard_map/slice | solution.py:25
  94.9 0.2 copy.63
  95.1 1.3 collective-permute-start.4
  96.4 0.2 copy.65
  96.5 4.3 %collective-permute-start.5 = (f32[384,1,256]{2,0,1:T(8,128)S(1)}, f32[384,1,256]{2,0,1:T(8,128)}, u32[]{:S(2)}, u32[]{:S(2)}) collective-permute-start(f32[384,1,256]{2,0,1:T(8,128)S(1)} %copy.65), channel_id=1, source_target_pairs={{0,1},{1,2},{2,3},{3,4},{4,5},{5,6},{6,7},{7,8},{8,9},{9,10},{10,1... | collective-permute-start | bytes 1179656 | tf_op jit(solution)/shard_map/ppermute | solution.py:14
  100.8 10.7 %fusion.33 = (f32[384,16,255]{0,2,1:T(8,128)}, f32[384,16,255]{0,2,1:T(8,128)}) fusion(f32[384,16,256]{0,2,1:T(8,128)} %get-tuple-element.30), kind=kLoop, calls=%fused_computation.62 | loop fusion | bytes 25067520 | tf_op jit(solution)/shard_map/slice | solution.py:25
  111.5 0.2 copy.64
  111.7 1.3 copy.66
  113.1 5.5 %maximum_multiply_fusion.1 = f32[384,18,256]{0,2,1:T(8,128)} fusion(f32[384,1,256]{0,2,1:T(8,128)S(1)} %copy.64, f32[384,16,256]{0,2,1:T(8,128)} %copy-done.1, f32[384,1,256]{0,2,1:T(8,128)S(1)} %copy.66, f32[384]{0:T(512)S(1)} %get-tuple-element.21, f32[18,256]{1,0:T(8,128)S(1)} %fusion.20), kind=kLoop, calls=%fused_computation.2 | loop fusion | flops 7077888 | bytes 14175744 | tf_op jit(solution)/shard_map/mul | solution.py:38
  118.6 0.1 slice-done.3
  118.7 17.3 %fusion.28 = (bf16[384,16,256]{0,2,1:T(8,128)(2,1)S(1)}, f32[384,16,256]{0,2,1:T(8,128)}) fusion(f32[384,16,255]{0,2,1:T(8,128)} %get-tuple-element.37, f32[384,16,255]{0,2,1:T(8,128)} %get-tuple-element.36, f32[384,18,256]{0,2,1:T(8,128)} %maximum_multiply_fusion.1, f32[384,16,256]{0,2,1:T(8,128)S(1)} %bitcast.21, f32[384,16,255]{0,2,1:T(8,128)} %get-tuple-element.33, ...), kind=kLoop, calls=%fused_computation.59 | loop fusion | flops 23592960 | bytes 54165504 | tf_op jit(solution)/shard_map/convert_element_type | solution.py:63
  136.0 1.7 copy-done.3
  137.7 12.1 %fusion.38 = f32[384,2048]{1,0:T(8,128)} fusion(bf16[384,4096]{0,1:T(8,128)(2,1)S(1)} %bitcast.22, bf16[4096,2048]{1,0:T(8,128)(2,1)} %param.12), kind=kOutput, calls=%fused_computation.67 | convolution fusion | flops 6442450944 | bytes 23068672 | tf_op jit(solution)/shard_map/dot_general | solution.py:64
  149.8 0.0 all-reduce.11.cloned.1.call-update
  149.8 0.0 all-reduce.13.cloned.1.call-start
  149.9 106.9 %all-reduce.11.cloned.1.call-done = f32[384,2048]{1,0:T(8,128)} async-done(((f32[384,2048]{1,0:T(8,128)}), f32[384,2048]{1,0:T(8,128)}) %all-reduce.11.cloned.1.call-update) | async-done | bytes 3145744 | tf_op jit(solution)/shard_map/psum | solution.py:65
  256.7 2.5 fusion.19
  259.2 2.3 fusion.23
  261.5 0.0 all-reduce.13.cloned.1.call-update
  261.6 6.7 %copy.69 = f32[384,16,256]{2,1,0:T(8,128)} copy(f32[384,16,256]{0,2,1:T(8,128)} %get-tuple-element.29) | data formatting | bytes 12582912
  268.3 0.2 convolution_reduce_fusion
  268.5 31.0 %psum.22 = f32[384]{0:T(512)} all-reduce(f32[384]{0:T(512)S(1)} %convolution_reduce_fusion), channel_id=1, replica_groups=mesh['groups'=2,'grid'=16] {'grid'}, use_global_device_ids=true, to_apply=%region_3.0 | all-reduce | flops 384 | bytes 3072 | tf_op jit(solution)/shard_map/psum | solution.py:71
  299.6 0.7 convolution_bitcast_fusion
  300.2 3.4 convolution_convert_fusion.1
  303.6 61.2 %all-reduce.13.cloned.1.call-done = f32[384,2048]{1,0:T(8,128)} async-done(((f32[384,2048]{1,0:T(8,128)}), f32[384,2048]{1,0:T(8,128)}) %all-reduce.13.cloned.1.call-update) | async-done | bytes 3145744 | tf_op jit(solution)/shard_map/psum | solution.py:82
  364.9 15.5 %convolution_convert_fusion = bf16[4096,2048]{1,0:T(8,128)(2,1)} fusion(bf16[384,4096]{0,1:T(8,128)(2,1)} %bitcast.23, f32[384,2048]{1,0:T(8,128)} %all-reduce.13.cloned.1.call-done, f32[384,2048]{1,0:T(8,128)} %all-reduce.11.cloned.1.call-done), kind=kOutput, calls=%fused_computation | convolution fusion | flops 6455558144 | bytes 26214400 | tf_op jit(solution)/shard_map/dot_general | solution.py:85
  (36 shorter events, 0.2 us)
Async XLA Ops:
  7.2 249.6 %copy-start = (bf16[2048,128]{1,0:T(8,128)(2,1)S(1)}, bf16[2048,128]{1,0:T(8,128)(2,1)}, u32[]{:S(2)}) copy-start(bf16[2048,128]{1,0:T(8,128)(2,1)} %param.13) | copy-start | bytes 1572868
  7.2 249.6 %all-reduce.11.cloned.1.call-start = ((), (), s32[]{:S(2)}) async-start(), calls=%async_computation | async-start | bytes 6291456 | tf_op jit(solution)/shard_map/psum | solution.py:65
  8.0 49.2 %collective-permute-start.2 = (f32[2,1,256]{2,1,0:T(1,128)S(1)}, f32[2,1,256]{2,1,0:T(1,128)S(1)}, u32[]{:S(2)}, u32[]{:S(2)}) collective-permute-start(f32[2,1,256]{2,1,0:T(1,128)S(1)} %get-tuple-element.44), channel_id=1, source_target_pairs={{0,1},{1,2},{2,3},{3,4},{4,5},{5,6},{6,7},{7,8},{8,9},{9,10},{10,1... | collective-permute-start | bytes 6152 | tf_op jit(solution)/shard_map/ppermute | solution.py:14
  10.4 46.8 %collective-permute-start.3 = (f32[2,1,256]{2,1,0:T(1,128)S(1)}, f32[2,1,256]{2,1,0:T(1,128)S(1)}, u32[]{:S(2)}, u32[]{:S(2)}) collective-permute-start(f32[2,1,256]{2,1,0:T(1,128)S(1)} %get-tuple-element.45), channel_id=1, source_target_pairs={{1,0},{2,1},{3,2},{4,3},{5,4},{6,5},{7,6},{8,7},{9,8},{10,9},{11,1... | collective-permute-start | bytes 6152 | tf_op jit(solution)/shard_map/ppermute | solution.py:17
  15.1 42.1 %collective-permute-start = (f32[384,1,256]{2,0,1:T(8,128)S(1)}, f32[384,1,256]{2,0,1:T(8,128)S(1)}, u32[]{:S(2)}, u32[]{:S(2)}) collective-permute-start(f32[384,1,256]{2,0,1:T(8,128)S(1)} %copy.70), channel_id=1, source_target_pairs={{1,0},{2,1},{3,2},{4,3},{5,4},{6,5},{7,6},{8,7},{9,8},{10,9},{11,1... | collective-permute-start | bytes 1179656 | tf_op jit(solution)/shard_map/ppermute | solution.py:17
  17.2 13.3 %copy-start.4 = (f32[2,16,256]{2,1,0:T(8,128)S(1)}, f32[2,16,256]{2,1,0:T(8,128)}, u32[]{:S(2)}) copy-start(f32[2,16,256]{2,1,0:T(8,128)} %param.9) | copy-start | bytes 98308
  17.2 13.3 %copy-start.7 = (s32[384,2]{0,1:T(2,128)S(1)}, s32[384,2]{0,1:T(2,128)}, u32[]{:S(2)}) copy-start(s32[384,2]{0,1:T(2,128)} %param.10) | copy-start | bytes 9220
  17.2 13.3 %copy-start.8 = (f32[8,2]{0,1:T(2,128)S(1)}, f32[8,2]{0,1:T(2,128)}, u32[]{:S(2)}) copy-start(f32[8,2]{0,1:T(2,128)} %param.11) | copy-start | bytes 196
  17.2 40.2 %collective-permute-start.1 = (f32[384,1,256]{2,0,1:T(8,128)}, f32[384,1,256]{2,0,1:T(8,128)}, u32[]{:S(2)}, u32[]{:S(2)}) collective-permute-start(f32[384,1,256]{2,0,1:T(8,128)} %copy.71), channel_id=1, source_target_pairs={{0,1},{1,2},{2,3},{3,4},{4,5},{5,6},{6,7},{7,8},{8,9},{9,10},{10,1... | collective-permute-start | bytes 1179656 | tf_op jit(solution)/shard_map/ppermute | solution.py:14
  57.2 7.5 %slice-start = ((s8[6291456]{0:T(1024)(128)(4,1)}), s8[2097152]{0:T(1024)(128)(4,1)S(1)}, s32[]{:S(2)}) async-start(s8[6291456]{0:T(1024)(128)(4,1)} %bitcast.18), calls=%async_computation.2 | async-start | bytes 4194304
  58.7 8.5 %slice-start.1 = ((s8[6291456]{0:T(1024)(128)(4,1)}), s8[4194304]{0:T(1024)(128)(4,1)S(1)}, s32[]{:S(2)}) async-start(s8[6291456]{0:T(1024)(128)(4,1)} %bitcast.18), calls=%async_computation.3 | async-start | bytes 8388608
  58.7 8.5 %copy-start.2 = (f32[384,16,255]{0,2,1:T(8,128)S(1)}, f32[384,16,255]{0,2,1:T(8,128)}, u32[]{:S(2)}) copy-start(f32[384,16,255]{0,2,1:T(8,128)} %get-tuple-element.38) | copy-start | bytes 18800644
  81.4 2.6 copy-start.1
  95.1 16.5 %collective-permute-start.4 = (f32[384,1,256]{2,0,1:T(8,128)S(1)}, f32[384,1,256]{2,0,1:T(8,128)S(1)}, u32[]{:S(2)}, u32[]{:S(2)}) collective-permute-start(f32[384,1,256]{2,0,1:T(8,128)S(1)} %copy.63), channel_id=1, source_target_pairs={{1,0},{2,1},{3,2},{4,3},{5,4},{6,5},{7,6},{8,7},{9,8},{10,9},{11,1... | collective-permute-start | bytes 1179656 | tf_op jit(solution)/shard_map/ppermute | solution.py:17
  96.5 15.2 %collective-permute-start.5 = (f32[384,1,256]{2,0,1:T(8,128)S(1)}, f32[384,1,256]{2,0,1:T(8,128)}, u32[]{:S(2)}, u32[]{:S(2)}) collective-permute-start(f32[384,1,256]{2,0,1:T(8,128)S(1)} %copy.65), channel_id=1, source_target_pairs={{0,1},{1,2},{2,3},{3,4},{4,5},{5,6},{6,7},{7,8},{8,9},{9,10},{10,1... | collective-permute-start | bytes 1179656 | tf_op jit(solution)/shard_map/ppermute | solution.py:14
  111.7 6.9 %slice-start.2 = ((s8[6291456]{0:T(1024)(128)(4,1)}), s8[2097152]{0:T(1024)(128)(4,1)S(1)}, s32[]{:S(2)}) async-start(s8[6291456]{0:T(1024)(128)(4,1)} %bitcast.20), calls=%async_computation.4 | async-start | bytes 4194304
  113.0 5.7 %slice-start.3 = ((s8[6291456]{0:T(1024)(128)(4,1)}), s8[4194304]{0:T(1024)(128)(4,1)S(1)}, s32[]{:S(2)}) async-start(s8[6291456]{0:T(1024)(128)(4,1)} %bitcast.20), calls=%async_computation.5 | async-start | bytes 8388608
  136.0 1.7 copy-start.3
  149.8 109.4 %copy-start.5 = (f32[384]{0:T(512)S(1)}, f32[384]{0:T(512)}, u32[]{:S(2)}) copy-start(f32[384]{0:T(512)} %param.15) | copy-start | bytes 4612
  149.8 109.4 %copy-start.6 = (f32[128]{0:T(128)S(1)}, f32[128]{0:T(128)}, u32[]{:S(2)}) copy-start(f32[128]{0:T(128)} %param.14) | copy-start | bytes 1540
  149.8 215.0 %all-reduce.13.cloned.1.call-start = ((), (), s32[]{:S(2)}) async-start(), calls=%async_computation.1 | async-start | bytes 6291456 | tf_op jit(solution)/shard_map/psum | solution.py:82
Sparse Core Ops, SparseCore 0:
  150.0 106.7 all-reduce.10
  261.7 103.1 all-reduce.12
where the time goes:
time: 388 us; the launch traced here: 387 us
  waiting for transfers between devices  168 us (43%)
  local copies, waits for them, and re-layouts  71.6 us (18%)
  other arithmetic  48.1 us (12%)
  matrix products  36.7 us (9%)
  blocking collectives  31 us (8%)
  starting transfers between devices  17.3 us (4%)
  between operations  14.3 us (4%)
    psum x1, waiting for transfers between devices, local(): first_pre = lax.psum(partial_first, 'grid')  107 us
    psum x1, waiting for transfers between devices, local(): back_raw = lax.psum(back_part, 'grid')  61.2 us
    slice x4, local copies, waits for them, and re-layouts, column_shift(): return jnp.concatenate([values[..., 1:], zero_col], axis=-1)  43.1 us
    psum x1, blocking collectives, local(): value = lax.psum(value_part, 'grid')  31 us
    unnamed x31, local copies, waits for them, and re-layouts  21 us
    mul x2, other arithmetic, kfe_step(): flux_y = velocity_y * centre  19.2 us
    convert_element_type x1, other arithmetic, local(): density.astype(jnp.bfloat16).reshape(scenarios, row_count * columns)  17.3 us
    dot_general x1, matrix products, local(): lax.dot_general(inputs, back_first, (((0,), (0,)), ((), ())), preferred_e...  15.5 us
  transfers between devices with their start and end apart: 8, of which 2 were waited for; matrix products, arithmetic and copies ran while one was open for 15% of the time, Pallas kernels for 0%

commit v1 on v0

--- a/solution.py
+++ b/solution.py
@@ -52,6 +52,10 @@
 
 
 def local(hist, drift, shocks, shock_table, first_weight, mid_weight, head_weight, cotangent):
+
+    def lead_squares(arr):
+        return lax.all_gather(arr, "grid").sum(axis=0)
+
     scenarios, row_count, columns = hist.shape
     step_count = shocks.shape[1]
     density = hist
@@ -79,7 +83,7 @@
     back_part = lax.dot_general(
         back_second, mid_weight, (((1,), (1,)), ((), ())), preferred_element_type=jnp.float32
     )
-    back_raw = lax.psum(back_part, "grid")
+    back_raw = lead_squares(back_part)
     first_f = first_act.astype(jnp.float32)
     back_first = (back_raw * (1.0 - first_f * first_f)).astype(jnp.bfloat16)
     grad_first = lax.dot_general(

time: 388 us -> 552 us (1.42)
  waiting for transfers between devices: 168 us -> 311 us
  other arithmetic: 48.1 us -> 67 us
    all_gather x0 -> x1, waiting for transfers between devices: none -> 203 us  [lead_squares(): return lax.all_gather(arr, 'grid').sum(axis=0)]
    psum x1 -> x0, waiting for transfers between devices: 61.2 us -> none  [local(): back_raw = lax.psum(back_part, 'grid')]
    reduce_sum x0 -> x1, other arithmetic: none -> 18.8 us  [lead_squares(): return lax.all_gather(arr, 'grid').sum(axis=0)]
  transfers between devices with their start and end apart: 8 -> 8, of which waited for: 2 -> 2; matrix products, arithmetic and copies ran while one was open for 15% -> 11% of each run, Pallas kernels for 0% -> 0%
where the time goes in v1:
time: 552 us; the launch traced here: 551 us
  waiting for transfers between devices  311 us (56%)
  local copies, waits for them, and re-layouts  72.7 us (13%)
  other arithmetic  67 us (12%)
  matrix products  36.7 us (7%)
  blocking collectives  32 us (6%)
  starting transfers between devices  17.2 us (3%)
  between operations  14.3 us (3%)
    all_gather x1, waiting for transfers between devices, lead_squares(): return lax.all_gather(arr, 'grid').sum(axis=0)  203 us
    psum x1, waiting for transfers between devices, local(): first_pre = lax.psum(partial_first, 'grid')  108 us
    slice x4, local copies, waits for them, and re-layouts, column_shift(): return jnp.concatenate([values[..., 1:], zero_col], axis=-1)  43.2 us
    psum x1, blocking collectives, local(): value = lax.psum(value_part, 'grid')  32 us
    unnamed x31, local copies, waits for them, and re-layouts  21.3 us
    mul x2, other arithmetic, kfe_step(): flux_y = velocity_y * centre  19.3 us
    reduce_sum x1, other arithmetic, lead_squares(): return lax.all_gather(arr, 'grid').sum(axis=0)  18.8 us
    convert_element_type x1, other arithmetic, local(): density.astype(jnp.bfloat16).reshape(scenarios, row_count * columns)  17.3 us
  transfers between devices with their start and end apart: 8, of which 2 were waited for; matrix products, arithmetic and copies ran while one was open for 11% of the time, Pallas kernels for 0%

profile of v1, /device:TPU:0, one launch (start us, length us, event | category | flops | bytes accessed | tf_op | source)
XLA Modules:
  0.0 551.1 jit_solution(6450237159370091917)
XLA Ops:
  7.2 0.0 all-reduce.10.cloned.1.call-start
  7.2 3.4 fusion.35
  10.7 1.3 collective-permute-start
  12.0 0.8 copy.71
  12.8 3.8 collective-permute-start.1
  16.6 0.7 fusion.37
  17.3 1.3 collective-permute-start.3
  18.6 4.4 collective-permute-start.2
  23.0 0.7 slice_bitcast_fusion
  23.7 6.6 %copy.58 = f32[384,16,256]{0,2,1:T(8,128)} copy(f32[384,16,256]{2,1,0:T(8,128)} %param.8) | data formatting | bytes 12582912 | tf_op args[0]
  30.4 0.1 multiply_reduce_fusion
  30.5 10.8 %fusion.34 = (f32[384,16,255]{0,2,1:T(8,128)}, f32[384,16,255]{0,2,1:T(8,128)}) fusion(f32[384,16,256]{0,2,1:T(8,128)} %copy.58), kind=kLoop, calls=%fused_computation.63 | loop fusion | bytes 25067520 | tf_op jit(solution)/shard_map/slice | solution.py:25
  41.3 4.9 add_multiply_fusion.1
  46.2 10.8 %fusion.36 = (f32[384,16,255]{0,2,1:T(8,128)}, f32[384,16,255]{0,2,1:T(8,128)}) fusion(f32[384,16,256]{0,2,1:T(8,128)} %add_multiply_fusion.1), kind=kLoop, calls=%fused_computation.65 | loop fusion | bytes 25067520 | tf_op jit(solution)/shard_map/slice | solution.py:25
  57.1 0.2 copy.51
  57.3 1.3 copy.53
  58.6 6.0 %maximum_multiply_fusion = f32[384,18,256]{0,2,1:T(8,128)} fusion(f32[384,1,256]{0,2,1:T(8,128)S(1)} %copy.51, f32[384,16,256]{0,2,1:T(8,128)} %copy.58, f32[384,1,256]{0,2,1:T(8,128)S(1)} %copy.53, f32[384]{0:T(512)S(1)} %get-tuple-element.25, f32[18,256]{1,0:T(8,128)S(1)} %fusion.20), kind=kLoop, calls=%fused_computation.1 | loop fusion | flops 7077888 | bytes 14175744 | tf_op jit(solution)/shard_map/mul | solution.py:38
  64.6 2.4 slice-done.1
  67.0 14.3 %add_multiply_fusion = (f32[384,16,256]{0,2,1:T(8,128)}, f32[384,16,256]{0,2,1:T(8,128)S(1)}) fusion(f32[384]{0:T(512)S(1)} %get-tuple-element.20, f32[16,256]{1,0:T(8,128)S(1)} %slice_bitcast_fusion, f32[384,16,255]{0,2,1:T(8,128)} %get-tuple-element.43, f32[384,16,255]{0,2,1:T(8,128)} %get-tuple-element.42, f32[384,18,256]{0,2,1:T(8,128)} %maximum_multiply_fusion, ...), kind=kLoop, calls=%fused_computation.27 | loop fusion | flops 25165824 | bytes 57329152 | tf_op jit(solution)/shard_map/mul | solution.py:40
  81.4 2.7 copy-done.1
  84.0 0.1 fusion.32
  84.1 10.8 %fusion.31 = (f32[384,16,255]{0,2,1:T(8,128)}, f32[384,16,255]{0,2,1:T(8,128)}) fusion(f32[384,16,256]{0,2,1:T(8,128)} %copy-done.1), kind=kLoop, calls=%fused_computation.60 | loop fusion | bytes 25067520 | tf_op jit(solution)/shard_map/slice | solution.py:25
  94.9 0.2 copy.63
  95.0 1.3 collective-permute-start.4
  96.3 0.2 copy.65
  96.5 5.0 collective-permute-start.5
  101.6 10.8 %fusion.33 = (f32[384,16,255]{0,2,1:T(8,128)}, f32[384,16,255]{0,2,1:T(8,128)}) fusion(f32[384,16,256]{0,2,1:T(8,128)} %get-tuple-element.30), kind=kLoop, calls=%fused_computation.62 | loop fusion | bytes 25067520 | tf_op jit(solution)/shard_map/slice | solution.py:25
  112.4 0.2 copy.64
  112.6 1.3 copy.66
  113.9 5.5 %maximum_multiply_fusion.1 = f32[384,18,256]{0,2,1:T(8,128)} fusion(f32[384,1,256]{0,2,1:T(8,128)S(1)} %copy.64, f32[384,16,256]{0,2,1:T(8,128)} %copy-done.1, f32[384,1,256]{0,2,1:T(8,128)S(1)} %copy.66, f32[384]{0:T(512)S(1)} %get-tuple-element.21, f32[18,256]{1,0:T(8,128)S(1)} %fusion.20), kind=kLoop, calls=%fused_computation.2 | loop fusion | flops 7077888 | bytes 14175744 | tf_op jit(solution)/shard_map/mul | solution.py:38
  119.4 0.1 slice-done.3
  119.5 17.3 %fusion.28 = (bf16[384,16,256]{0,2,1:T(8,128)(2,1)S(1)}, f32[384,16,256]{0,2,1:T(8,128)}) fusion(f32[384,16,255]{0,2,1:T(8,128)} %get-tuple-element.37, f32[384,16,255]{0,2,1:T(8,128)} %get-tuple-element.36, f32[384,18,256]{0,2,1:T(8,128)} %maximum_multiply_fusion.1, f32[384,16,256]{0,2,1:T(8,128)S(1)} %bitcast.22, f32[384,16,255]{0,2,1:T(8,128)} %get-tuple-element.33, ...), kind=kLoop, calls=%fused_computation.59 | loop fusion | flops 23592960 | bytes 54165504 | tf_op jit(solution)/shard_map/convert_element_type | solution.py:67
  136.8 1.6 copy-done.3
  138.4 12.1 %fusion.38 = f32[384,2048]{1,0:T(8,128)} fusion(bf16[384,4096]{0,1:T(8,128)(2,1)S(1)} %bitcast.24, bf16[4096,2048]{1,0:T(8,128)(2,1)} %param.12), kind=kOutput, calls=%fused_computation.67 | convolution fusion | flops 6442450944 | bytes 23068672 | tf_op jit(solution)/shard_map/dot_general | solution.py:68
  150.5 0.0 all-reduce.10.cloned.1.call-update
  150.6 0.0 all-gather.3.cloned.1.call-start
  150.6 107.8 %all-reduce.10.cloned.1.call-done = f32[384,2048]{1,0:T(8,128)} async-done(((f32[384,2048]{1,0:T(8,128)}), f32[384,2048]{1,0:T(8,128)}) %all-reduce.10.cloned.1.call-update) | async-done | bytes 3145744 | tf_op jit(solution)/shard_map/psum | solution.py:69
  258.5 2.5 fusion.19
  261.0 2.3 fusion.23
  263.2 0.0 all-gather.3.cloned.1.call-update
  263.3 7.0 %copy.69 = f32[384,16,256]{2,1,0:T(8,128)} copy(f32[384,16,256]{0,2,1:T(8,128)} %get-tuple-element.29) | data formatting | bytes 12582912
  270.3 0.2 convolution_reduce_fusion
  270.5 32.0 %psum.15 = f32[384]{0:T(512)} all-reduce(f32[384]{0:T(512)S(1)} %convolution_reduce_fusion), channel_id=1, replica_groups=mesh['groups'=2,'grid'=16] {'grid'}, use_global_device_ids=true, to_apply=%region_3.0 | all-reduce | flops 384 | bytes 3072 | tf_op jit(solution)/shard_map/psum | solution.py:75
  302.5 0.7 convolution_bitcast_fusion
  303.2 3.4 convolution_convert_fusion.1
  306.6 203.4 %all-gather.3.cloned.1.call-done = f32[6144,2048]{1,0:T(8,128)} async-done(((f32[384,2048]{1,0:T(8,128)}), f32[6144,2048]{1,0:T(8,128)}) %all-gather.3.cloned.1.call-update) | async-done | bytes 50331664 | tf_op jit(solution)/shard_map/all_gather | solution.py:57
  510.0 18.8 %reduce_sum.29 = f32[384,2048]{1,0:T(8,128)} reduce(f32[16,384,2048]{2,1,0:T(8,128)} %bitcast.23, f32[]{:T(128)} %constant.5.clone.1), dimensions={0}, to_apply=%region_4.0 | reduce | flops 11796480 | bytes 53477380 | tf_op jit(solution)/shard_map/reduce_sum | solution.py:57
  528.8 15.5 %convolution_convert_fusion = bf16[4096,2048]{1,0:T(8,128)(2,1)} fusion(bf16[384,4096]{0,1:T(8,128)(2,1)} %bitcast.25, f32[384,2048]{1,0:T(8,128)} %reduce_sum.29, f32[384,2048]{1,0:T(8,128)} %all-reduce.10.cloned.1.call-done), kind=kOutput, calls=%fused_computation | convolution fusion | flops 6455558144 | bytes 26214400 | tf_op jit(solution)/shard_map/dot_general | solution.py:89
  (37 shorter events, 0.2 us)
Async XLA Ops:
  7.2 251.3 %copy-start = (bf16[2048,128]{1,0:T(8,128)(2,1)S(1)}, bf16[2048,128]{1,0:T(8,128)(2,1)}, u32[]{:S(2)}) copy-start(bf16[2048,128]{1,0:T(8,128)(2,1)} %param.13) | copy-start | bytes 1572868
  7.2 251.3 %all-reduce.10.cloned.1.call-start = ((), (), s32[]{:S(2)}) async-start(), calls=%async_computation | async-start | bytes 6291456 | tf_op jit(solution)/shard_map/psum | solution.py:69
  10.7 46.4 %collective-permute-start = (f32[384,1,256]{2,0,1:T(8,128)S(1)}, f32[384,1,256]{2,0,1:T(8,128)S(1)}, u32[]{:S(2)}, u32[]{:S(2)}) collective-permute-start(f32[384,1,256]{2,0,1:T(8,128)S(1)} %copy.70), channel_id=1, source_target_pairs={{1,0},{2,1},{3,2},{4,3},{5,4},{6,5},{7,6},{8,7},{9,8},{10,9},{11,1... | collective-permute-start | bytes 1179656 | tf_op jit(solution)/shard_map/ppermute | solution.py:17
  12.8 44.5 %collective-permute-start.1 = (f32[384,1,256]{2,0,1:T(8,128)}, f32[384,1,256]{2,0,1:T(8,128)}, u32[]{:S(2)}, u32[]{:S(2)}) collective-permute-start(f32[384,1,256]{2,0,1:T(8,128)} %copy.71), channel_id=1, source_target_pairs={{0,1},{1,2},{2,3},{3,4},{4,5},{5,6},{6,7},{7,8},{8,9},{9,10},{10,1... | collective-permute-start | bytes 1179656 | tf_op jit(solution)/shard_map/ppermute | solution.py:14
  17.3 39.7 %collective-permute-start.3 = (f32[2,1,256]{2,1,0:T(1,128)S(1)}, f32[2,1,256]{2,1,0:T(1,128)S(1)}, u32[]{:S(2)}, u32[]{:S(2)}) collective-permute-start(f32[2,1,256]{2,1,0:T(1,128)S(1)} %get-tuple-element.45), channel_id=1, source_target_pairs={{1,0},{2,1},{3,2},{4,3},{5,4},{6,5},{7,6},{8,7},{9,8},{10,9},{11,1... | collective-permute-start | bytes 6152 | tf_op jit(solution)/shard_map/ppermute | solution.py:17
  18.6 38.4 %collective-permute-start.2 = (f32[2,1,256]{2,1,0:T(1,128)S(1)}, f32[2,1,256]{2,1,0:T(1,128)S(1)}, u32[]{:S(2)}, u32[]{:S(2)}) collective-permute-start(f32[2,1,256]{2,1,0:T(1,128)S(1)} %get-tuple-element.44), channel_id=1, source_target_pairs={{0,1},{1,2},{2,3},{3,4},{4,5},{5,6},{6,7},{7,8},{8,9},{9,10},{10,1... | collective-permute-start | bytes 6152 | tf_op jit(solution)/shard_map/ppermute | solution.py:14
  23.7 6.6 %copy-start.7 = (s32[384,2]{0,1:T(2,128)S(1)}, s32[384,2]{0,1:T(2,128)}, u32[]{:S(2)}) copy-start(s32[384,2]{0,1:T(2,128)} %param.10) | copy-start | bytes 9220
  23.7 6.6 %copy-start.8 = (f32[8,2]{0,1:T(2,128)S(1)}, f32[8,2]{0,1:T(2,128)}, u32[]{:S(2)}) copy-start(f32[8,2]{0,1:T(2,128)} %param.11) | copy-start | bytes 196
  46.2 10.8 %copy-start.4 = (f32[2,16,256]{2,1,0:T(8,128)S(1)}, f32[2,16,256]{2,1,0:T(8,128)}, u32[]{:S(2)}) copy-start(f32[2,16,256]{2,1,0:T(8,128)} %param.9) | copy-start | bytes 98308
  57.1 7.5 %slice-start = ((s8[6291456]{0:T(1024)(128)(4,1)}), s8[2097152]{0:T(1024)(128)(4,1)S(1)}, s32[]{:S(2)}) async-start(s8[6291456]{0:T(1024)(128)(4,1)} %bitcast.19), calls=%async_computation.2 | async-start | bytes 4194304
  58.5 8.5 %slice-start.1 = ((s8[6291456]{0:T(1024)(128)(4,1)}), s8[4194304]{0:T(1024)(128)(4,1)S(1)}, s32[]{:S(2)}) async-start(s8[6291456]{0:T(1024)(128)(4,1)} %bitcast.19), calls=%async_computation.3 | async-start | bytes 8388608
  58.5 8.5 %copy-start.2 = (f32[384,16,255]{0,2,1:T(8,128)S(1)}, f32[384,16,255]{0,2,1:T(8,128)}, u32[]{:S(2)}) copy-start(f32[384,16,255]{0,2,1:T(8,128)} %get-tuple-element.38) | copy-start | bytes 18800644
  81.4 2.7 copy-start.1
  95.0 17.3 %collective-permute-start.4 = (f32[384,1,256]{2,0,1:T(8,128)S(1)}, f32[384,1,256]{2,0,1:T(8,128)S(1)}, u32[]{:S(2)}, u32[]{:S(2)}) collective-permute-start(f32[384,1,256]{2,0,1:T(8,128)S(1)} %copy.63), channel_id=1, source_target_pairs={{1,0},{2,1},{3,2},{4,3},{5,4},{6,5},{7,6},{8,7},{9,8},{10,9},{11,1... | collective-permute-start | bytes 1179656 | tf_op jit(solution)/shard_map/ppermute | solution.py:17
  96.5 16.0 %collective-permute-start.5 = (f32[384,1,256]{2,0,1:T(8,128)S(1)}, f32[384,1,256]{2,0,1:T(8,128)}, u32[]{:S(2)}, u32[]{:S(2)}) collective-permute-start(f32[384,1,256]{2,0,1:T(8,128)S(1)} %copy.65), channel_id=1, source_target_pairs={{0,1},{1,2},{2,3},{3,4},{4,5},{5,6},{6,7},{7,8},{8,9},{9,10},{10,1... | collective-permute-start | bytes 1179656 | tf_op jit(solution)/shard_map/ppermute | solution.py:14
  112.5 6.9 %slice-start.2 = ((s8[6291456]{0:T(1024)(128)(4,1)}), s8[2097152]{0:T(1024)(128)(4,1)S(1)}, s32[]{:S(2)}) async-start(s8[6291456]{0:T(1024)(128)(4,1)} %bitcast.21), calls=%async_computation.4 | async-start | bytes 4194304
  113.9 5.7 %slice-start.3 = ((s8[6291456]{0:T(1024)(128)(4,1)}), s8[4194304]{0:T(1024)(128)(4,1)S(1)}, s32[]{:S(2)}) async-start(s8[6291456]{0:T(1024)(128)(4,1)} %bitcast.21), calls=%async_computation.5 | async-start | bytes 8388608
  136.8 1.6 copy-start.3
  150.5 110.4 %copy-start.5 = (f32[384]{0:T(512)S(1)}, f32[384]{0:T(512)}, u32[]{:S(2)}) copy-start(f32[384]{0:T(512)} %param.15) | copy-start | bytes 4612
  150.5 110.4 %copy-start.6 = (f32[128]{0:T(128)S(1)}, f32[128]{0:T(128)}, u32[]{:S(2)}) copy-start(f32[128]{0:T(128)} %param.14) | copy-start | bytes 1540
  150.6 359.4 %all-gather.3.cloned.1.call-start = ((), (), s32[]{:S(2)}) async-start(), calls=%async_computation.1 | async-start | bytes 53477376 | tf_op jit(solution)/shard_map/all_gather | solution.py:57
Sparse Core Ops, SparseCore 0:
  150.7 107.7 all-reduce.9
  263.4 246.5 all-gather.2
